TPU v7x, 32 devices: a whole 2x2x4 slice. The times are simulated.
32 devices in a mesh: wide: 16 (over z, y, x), narrow: 2 (over core).
Axes of the slice: x: 2, y: 2, z: 4, core: 2. Of those that a mesh axis runs over, the one named last changes fastest.
Arguments:
- passages: bfloat16 [16384, 768], P('wide'), may hold values from -32 to 32
- centroids: bfloat16 [4096, 768], P('narrow'), may hold values from -6 to 6
Outputs:
- new_centroids: float32 [4096, 768], P('narrow')
- row_potential: float32 [16384], P('wide')
- col_potential: float32 [4096], P('narrow')
All inputs are finite; a program needn't handle non-finite values.
Results may differ from a plain program's by a relative error of at most 0.00035.
Values sent between devices are 32-bit elements; how exact they have to be, the bound alone decides.
A program may use at most 64 MiB of HBM per device.

v0:
```python
import jax
import jax.numpy as jnp
from jax import lax
from jax.sharding import PartitionSpec as P

VECTOR_DIMENSION = 768
CENTROIDS = 4096
SWEEPS = 3
entropic_regularizer = 0.02


def inverse_rms(values):
    wide_values = values.astype(jnp.float32)
    return lax.rsqrt(jnp.mean(wide_values * wide_values, axis=1) + 1e-06)


def unit_rows(totals):
    return totals * lax.rsqrt(jnp.mean(totals * totals, axis=1, keepdims=True) + 1e-06)


def body(passages, centroids):
    passage_row_scale = inverse_rms(passages)
    cluster_center_factor = inverse_rms(centroids)
    cosine_affinity_matrix = lax.dot_general(
        passages, centroids, (((1,), (1,)), ((), ())), preferred_element_type=jnp.float32
    )
    kernel = jnp.exp(
        cosine_affinity_matrix
        * passage_row_scale[:, None]
        * cluster_center_factor[None, :]
        * (1.0 / (VECTOR_DIMENSION * entropic_regularizer))
    )
    target = float(lax.axis_size("wide") * passages.shape[0]) / float(
        lax.axis_size("narrow") * centroids.shape[0]
    )
    col_factor = jnp.ones((centroids.shape[0],), jnp.float32)
    row_factor = jnp.ones((passages.shape[0],), jnp.float32)
    for number in range(SWEEPS):
        row_part = jnp.dot(kernel, col_factor, precision=lax.Precision.HIGHEST)
        row_factor = 1.0 / lax.psum(row_part, "narrow")
        col_part = jnp.dot(row_factor, kernel, precision=lax.Precision.HIGHEST)
        col_factor = target / lax.psum(col_part, "wide")
    weights = (
        row_factor[:, None] * kernel * col_factor[None, :] * passage_row_scale[:, None]
    ).astype(jnp.bfloat16)
    partial_sums = lax.dot_general(
        weights, passages, (((0,), (0,)), ((), ())), preferred_element_type=jnp.float32
    )
    new_centroids = unit_rows(lax.psum(partial_sums, "wide"))
    row_potential = jnp.log(CENTROIDS * row_factor)
    return (new_centroids, row_potential, jnp.log(col_factor))


def solution(mesh):
    in_specs = (P("wide", None), P("narrow", None))
    out_specs = (P("narrow", None), P("wide"), P("narrow"))
    return jax.shard_map(body, mesh=mesh, in_specs=in_specs, out_specs=out_specs, check_vma=False)
```

profile of v0, /device:TPU:0, one launch (start us, length us, event | category | flops | bytes accessed | tf_op | source)
XLA Modules:
  0.0 426.3 jit_solution(12740581471887425097)
XLA Ops:
  7.2 0.0 all-reduce.2.cloned.1.call-start
  7.2 1.8 multiply_reduce_fusion.2
  9.0 2.6 multiply_reduce_fusion.1
  11.6 6.0 %multiply_exponential_fusion = f32[1024,2048]{1,0:T(8,128)S(1)} fusion(bf16[1024,768]{1,0:T(8,128)(2,1)} %param.2, bf16[2048,768]{1,0:T(8,128)(2,1)} %param.3, f32[2048]{0:T(1024)S(1)} %add_rsqrt_fusion.1, f32[1024]{0:T(1024)S(1)} %add_rsqrt_fusion.2), kind=kOutput, calls=%fused_computation.1 | convolution fusion | flops 3227516928 | bytes 13119488 | tf_op jit(solution)/shard_map/dot_general | solution.py:24
  17.6 3.2 copy-done
  20.8 7.1 %fusion.4 = f32[1,1024]{1,0:T(1,128)S(1)} fusion(f32[1024,2048]{1,0:T(8,128)S(1)} %multiply_exponential_fusion), kind=kOutput, calls=%fused_computation.12 | convolution fusion | flops 25165824 | bytes 8392704 | tf_op jit(solution)/shard_map/dot_general | solution.py:39
  28.0 2.6 psum.49
  30.6 6.3 %fusion.8 = f32[1,2048]{1,0:T(1,128)S(1)} fusion(f32[1024,1]{0,1:T(1,128)S(1)} %bitcast.31, f32[1024,2048]{1,0:T(8,128)} %copy-done), kind=kOutput, calls=%fused_computation.24 | convolution fusion | flops 25165824 | bytes 8400896 | tf_op jit(solution)/shard_map/dot_general | solution.py:41
  36.9 44.0 %psum.50 = f32[2048]{0:T(1024)S(1)} all-reduce(f32[2048]{0:T(1024)S(1)} %bitcast.25), channel_id=1, replica_groups=mesh['wide'=16,'narrow'=2] {'wide'}, use_global_device_ids=true, to_apply=%region_3.0 | all-reduce | flops 2048 | bytes 16384 | tf_op jit(solution)/shard_map/psum | solution.py:42
  81.0 9.4 %fusion.9 = f32[1,1024]{1,0:T(1,128)S(1)} fusion(f32[1024,2048]{1,0:T(8,128)} %copy-done, f32[2048,1]{0,1:T(1,128)S(1)} %bitcast.26), kind=kOutput, calls=%fused_computation.25 | convolution fusion | flops 25165824 | bytes 8400896 | tf_op jit(solution)/shard_map/dot_general | solution.py:39
  90.4 2.5 psum.51
  92.9 6.3 %fusion.10 = f32[1,2048]{1,0:T(1,128)S(1)} fusion(f32[1024,1]{0,1:T(1,128)S(1)} %bitcast.33, f32[1024,2048]{1,0:T(8,128)} %copy-done), kind=kOutput, calls=%fused_computation.26 | convolution fusion | flops 25165824 | bytes 8400896 | tf_op jit(solution)/shard_map/dot_general | solution.py:41
  99.2 37.1 %psum.52 = f32[2048]{0:T(1024)S(1)} all-reduce(f32[2048]{0:T(1024)S(1)} %bitcast.27), channel_id=1, replica_groups=mesh['wide'=16,'narrow'=2] {'wide'}, use_global_device_ids=true, to_apply=%region_5.0 | all-reduce | flops 2048 | bytes 16384 | tf_op jit(solution)/shard_map/psum | solution.py:42
  136.3 9.5 %fusion.11 = f32[1,1024]{1,0:T(1,128)S(1)} fusion(f32[1024,2048]{1,0:T(8,128)} %copy-done, f32[2048,1]{0,1:T(1,128)S(1)} %bitcast.28), kind=kOutput, calls=%fused_computation.27 | convolution fusion | flops 25165824 | bytes 8400896 | tf_op jit(solution)/shard_map/dot_general | solution.py:39
  145.8 2.5 psum.53
  148.3 0.6 multiply_log_fusion
  148.9 6.3 %fusion.12 = f32[1,2048]{1,0:T(1,128)S(1)} fusion(f32[1024,1]{0,1:T(1,128)S(1)} %bitcast.30, f32[1024,2048]{1,0:T(8,128)} %copy-done), kind=kOutput, calls=%fused_computation.28 | convolution fusion | flops 25165824 | bytes 8400896 | tf_op jit(solution)/shard_map/dot_general | solution.py:41
  155.2 39.3 %psum.54 = f32[2048]{0:T(1024)S(1)} all-reduce(f32[2048]{0:T(1024)S(1)} %bitcast.29), channel_id=1, replica_groups=mesh['wide'=16,'narrow'=2] {'wide'}, use_global_device_ids=true, to_apply=%region_7.0 | all-reduce | flops 2048 | bytes 16384 | tf_op jit(solution)/shard_map/psum | solution.py:42
  194.6 0.6 fusion.7
  195.2 10.1 %fusion = f32[2048,768]{1,0:T(8,128)} fusion(bf16[1024,768]{1,0:T(8,128)(2,1)S(1)} %copy-done.2, f32[1024,2048]{1,0:T(8,128)} %copy-done, f32[2048]{0:T(1024)S(1)} %get-tuple-element.4, f32[1024]{0:T(1024)S(1)} %get-tuple-element.6, f32[1024]{0:T(1024)S(1)} %add_rsqrt_fusion.2), kind=kOutput, calls=%fused_computation.4 | convolution fusion | flops 3229614080 | bytes 16269312 | tf_op jit(solution)/shard_map/dot_general | solution.py:46
  205.3 206.4 %all-reduce.2.cloned.1.call-done = f32[2048,768]{1,0:T(8,128)} async-done(((f32[2048,768]{1,0:T(8,128)}), f32[2048,768]{1,0:T(8,128)}) %all-reduce.2.cloned.1.call-update) | async-done | bytes 6291472 | tf_op jit(solution)/shard_map/psum | solution.py:49
  411.7 3.4 multiply_reduce_fusion
  415.1 1.2 copy-done.1
  416.3 3.2 broadcast_multiply_fusion
  (12 shorter events, 0.1 us)
Async XLA Ops:
  7.2 404.5 %all-reduce.2.cloned.1.call-start = ((), (), s32[]{:S(2)}) async-start(), calls=%async_computation | async-start | bytes 12582912 | tf_op jit(solution)/shard_map/psum | solution.py:49
  17.6 3.2 copy-start
  136.3 58.9 %copy-start.2 = (bf16[1024,768]{1,0:T(8,128)(2,1)S(1)}, bf16[1024,768]{1,0:T(8,128)(2,1)}, u32[]{:S(2)}) copy-start(bf16[1024,768]{1,0:T(8,128)(2,1)} %param.2) | copy-start | bytes 4718596
  411.7 4.6 %copy-start.1 = (f32[2048,768]{1,0:T(8,128)S(1)}, f32[2048,768]{1,0:T(8,128)}, u32[]{:S(2)}) copy-start(f32[2048,768]{1,0:T(8,128)} %all-reduce.2.cloned.1.call-done) | copy-start | bytes 18874372
Sparse Core Ops, SparseCore 0:
  205.4 206.2 all-reduce.1
where the time goes:
time: 427 us; the launch traced here: 426 us
  waiting for transfers between devices  206 us (48%)
  blocking collectives  128 us (30%)
  matrix products  61.2 us (14%)
  between operations  14.1 us (3%)
  other arithmetic  12.2 us (3%)
  local copies, waits for them, and re-layouts  4.39 us (1%)
    psum x1, waiting for transfers between devices, body(): new_centroids = unit_rows(lax.psum(partial_sums, 'wide'))  206 us
    psum x3, blocking collectives, body(): col_factor = target / lax.psum(col_part, 'wide')  120 us
    dot_general x3, matrix products, body(): row_part = jnp.dot(kernel, col_factor, precision=lax.Precision.HIGHEST)  26 us
    dot_general x3, matrix products, body(): col_part = jnp.dot(row_factor, kernel, precision=lax.Precision.HIGHEST)  19 us
    dot_general x1, matrix products, body(): lax.dot_general(weights, passages, (((0,), (0,)), ((), ())), preferred_el...  10.1 us
  transfers between devices with their start and end apart: 1, of which 1 were waited for; matrix products, arithmetic and copies ran while one was open for 0% of the time, Pallas kernels for 0%

commit v1 on v0

--- a/solution.py
+++ b/solution.py
@@ -39,7 +39,7 @@
         row_part = jnp.dot(kernel, col_factor, precision=lax.Precision.HIGHEST)
         row_factor = 1.0 / lax.psum(row_part, "narrow")
         col_part = jnp.dot(row_factor, kernel, precision=lax.Precision.HIGHEST)
-        col_factor = target / lax.psum(col_part, "wide")
+        col_factor = target / jnp.sum(lax.all_gather(col_part, "wide"), axis=0)
     weights = (
         row_factor[:, None] * kernel * col_factor[None, :] * passage_row_scale[:, None]
     ).astype(jnp.bfloat16)

time: 427 us -> 424 us (level)
    psum x3 -> x0, blocking collectives: 120 us -> none  [body(): col_factor = target / lax.psum(col_part, 'wide')]
    all_gather x0 -> x3, blocking collectives: none -> 118 us  [body(): col_factor = target / jnp.sum(lax.all_gather(col_part, 'wide'), axis=0)]
where the time goes in v1:
time: 424 us
  waiting for transfers between devices  206 us (49%)
  blocking collectives  125 us (29%)
  matrix products  61.2 us (14%)
  between operations  14.1 us (3%)
  other arithmetic  12.3 us (3%)
  local copies, waits for them, and re-layouts  4.47 us (1%)
    psum x1, waiting for transfers between devices, body(): new_centroids = unit_rows(lax.psum(partial_sums, 'wide'))  206 us
    all_gather x3, blocking collectives, body(): col_factor = target / jnp.sum(lax.all_gather(col_part, 'wide'), axis=0)  118 us
    dot_general x3, matrix products, body(): row_part = jnp.dot(kernel, col_factor, precision=lax.Precision.HIGHEST)  26 us
    dot_general x3, matrix products, body(): col_part = jnp.dot(row_factor, kernel, precision=lax.Precision.HIGHEST)  19 us
    dot_general x1, matrix products, body(): lax.dot_general(weights, passages, (((0,), (0,)), ((), ())), preferred_el...  10.1 us
  transfers between devices with their start and end apart: 1, of which 1 were waited for; matrix products, arithmetic and copies ran while one was open for 0% of the time, Pallas kernels for 0%

profile of v1, /device:TPU:0, one launch (start us, length us, event | category | flops | bytes accessed | tf_op | source)
XLA Modules:
  0.0 423.6 jit_solution(8781552148967216192)
XLA Ops:
  7.2 0.0 all-reduce.2.cloned.1.call-start
  7.2 1.8 multiply_reduce_fusion.2
  9.0 2.6 multiply_reduce_fusion.1
  11.6 6.0 %multiply_exponential_fusion = f32[1024,2048]{1,0:T(8,128)S(1)} fusion(bf16[1024,768]{1,0:T(8,128)(2,1)} %param.2, bf16[2048,768]{1,0:T(8,128)(2,1)} %param.3, f32[2048]{0:T(1024)S(1)} %add_rsqrt_fusion.1, f32[1024]{0:T(1024)S(1)} %add_rsqrt_fusion.2), kind=kOutput, calls=%fused_computation.1 | convolution fusion | flops 3227516928 | bytes 13119488 | tf_op jit(solution)/shard_map/dot_general | solution.py:24
  17.6 3.2 copy-done
  20.8 7.1 %fusion.4 = f32[1,1024]{1,0:T(1,128)S(1)} fusion(f32[1024,2048]{1,0:T(8,128)S(1)} %multiply_exponential_fusion), kind=kOutput, calls=%fused_computation.12 | convolution fusion | flops 25165824 | bytes 8392704 | tf_op jit(solution)/shard_map/dot_general | solution.py:39
  28.0 2.6 psum.28
  30.6 6.3 %fusion.8 = f32[1,2048]{1,0:T(1,128)S(1)} fusion(f32[1024,1]{0,1:T(1,128)S(1)} %bitcast.31, f32[1024,2048]{1,0:T(8,128)} %copy-done), kind=kOutput, calls=%fused_computation.24 | convolution fusion | flops 25165824 | bytes 8400896 | tf_op jit(solution)/shard_map/dot_general | solution.py:41
  36.9 43.1 %all-gather = f32[32768]{0:T(1024)S(1)} all-gather(f32[2048]{0:T(1024)S(1)} %bitcast.25), channel_id=2, replica_groups=mesh['wide'=16,'narrow'=2] {'wide'}, dimensions={0}, use_global_device_ids=true | all-gather | bytes 139264 | tf_op jit(solution)/shard_map/all_gather | solution.py:42
  80.1 9.4 %fusion.9 = f32[1,1024]{1,0:T(1,128)S(1)} fusion(f32[1024,2048]{1,0:T(8,128)} %copy-done, f32[2048,1]{0,1:T(1,128)S(1)} %bitcast.28), kind=kOutput, calls=%fused_computation.25 | convolution fusion | flops 25165824 | bytes 8400896 | tf_op jit(solution)/shard_map/dot_general | solution.py:39
  89.5 2.5 psum.29
  92.0 6.3 %fusion.10 = f32[1,2048]{1,0:T(1,128)S(1)} fusion(f32[1024,1]{0,1:T(1,128)S(1)} %bitcast.33, f32[1024,2048]{1,0:T(8,128)} %copy-done), kind=kOutput, calls=%fused_computation.26 | convolution fusion | flops 25165824 | bytes 8400896 | tf_op jit(solution)/shard_map/dot_general | solution.py:41
  98.4 36.1 %all-gather.1 = f32[32768]{0:T(1024)S(1)} all-gather(f32[2048]{0:T(1024)S(1)} %bitcast.26), channel_id=3, replica_groups=mesh['wide'=16,'narrow'=2] {'wide'}, dimensions={0}, use_global_device_ids=true | all-gather | bytes 139264 | tf_op jit(solution)/shard_map/all_gather | solution.py:42
  134.6 9.5 %fusion.11 = f32[1,1024]{1,0:T(1,128)S(1)} fusion(f32[1024,2048]{1,0:T(8,128)} %copy-done, f32[2048,1]{0,1:T(1,128)S(1)} %bitcast.29), kind=kOutput, calls=%fused_computation.27 | convolution fusion | flops 25165824 | bytes 8400896 | tf_op jit(solution)/shard_map/dot_general | solution.py:39
  144.1 2.5 psum.30
  146.6 0.6 multiply_log_fusion
  147.2 6.3 %fusion.12 = f32[1,2048]{1,0:T(1,128)S(1)} fusion(f32[1024,1]{0,1:T(1,128)S(1)} %bitcast.30, f32[1024,2048]{1,0:T(8,128)} %copy-done), kind=kOutput, calls=%fused_computation.28 | convolution fusion | flops 25165824 | bytes 8400896 | tf_op jit(solution)/shard_map/dot_general | solution.py:41
  153.5 38.4 %all-gather.2 = f32[32768]{0:T(1024)S(1)} all-gather(f32[2048]{0:T(1024)S(1)} %bitcast.27), channel_id=4, replica_groups=mesh['wide'=16,'narrow'=2] {'wide'}, dimensions={0}, use_global_device_ids=true | all-gather | bytes 139264 | tf_op jit(solution)/shard_map/all_gather | solution.py:42
  191.9 0.6 fusion.7
  192.6 10.1 %fusion = f32[2048,768]{1,0:T(8,128)} fusion(bf16[1024,768]{1,0:T(8,128)(2,1)S(1)} %copy-done.2, f32[1024,2048]{1,0:T(8,128)} %copy-done, f32[2048]{0:T(1024)S(1)} %get-tuple-element.4, f32[1024]{0:T(1024)S(1)} %get-tuple-element.6, f32[1024]{0:T(1024)S(1)} %add_rsqrt_fusion.2), kind=kOutput, calls=%fused_computation.4 | convolution fusion | flops 3229614080 | bytes 16269312 | tf_op jit(solution)/shard_map/dot_general | solution.py:46
  202.7 206.3 %all-reduce.2.cloned.1.call-done = f32[2048,768]{1,0:T(8,128)} async-done(((f32[2048,768]{1,0:T(8,128)}), f32[2048,768]{1,0:T(8,128)}) %all-reduce.2.cloned.1.call-update) | async-done | bytes 6291472 | tf_op jit(solution)/shard_map/psum | solution.py:49
  409.0 3.4 multiply_reduce_fusion
  412.4 1.2 copy-done.1
  413.6 3.2 broadcast_multiply_fusion
  (18 shorter events, 0.2 us)
Async XLA Ops:
  7.2 401.8 %all-reduce.2.cloned.1.call-start = ((), (), s32[]{:S(2)}) async-start(), calls=%async_computation | async-start | bytes 12582912 | tf_op jit(solution)/shard_map/psum | solution.py:49
  17.6 3.2 copy-start
  134.6 58.0 %copy-start.2 = (bf16[1024,768]{1,0:T(8,128)(2,1)S(1)}, bf16[1024,768]{1,0:T(8,128)(2,1)}, u32[]{:S(2)}) copy-start(bf16[1024,768]{1,0:T(8,128)(2,1)} %param.2) | copy-start | bytes 4718596
  409.0 4.6 %copy-start.1 = (f32[2048,768]{1,0:T(8,128)S(1)}, f32[2048,768]{1,0:T(8,128)}, u32[]{:S(2)}) copy-start(f32[2048,768]{1,0:T(8,128)} %all-reduce.2.cloned.1.call-done) | copy-start | bytes 18874372
Sparse Core Ops, SparseCore 0:
  202.8 206.1 all-reduce.1
